TPU v7x, 32 devices: a whole 2x2x4 slice. The times are simulated.
32 devices in a mesh: resp: 2 (over y), item: 16 (over z, x, core).
Axes of the slice: x: 2, y: 2, z: 4, core: 2. Of those that a mesh axis runs over, the one named last changes fastest.
Arguments:
- coupling: bfloat16 [2, 4096, 2048], P('resp', 'item'), may hold values from -6 to 6
- noise: bfloat16 [2, 4096, 2048], P('resp', 'item'), may hold values from -6 to 6
- bias: float32 [16, 256], P('item', 'resp'), may hold values from -4 to 4
- responses: int32 [1024, 4096], P(None, 'item'), may hold values 0 or 1
- indices: int32 [512], replicated, may hold values from 0 to 1023
Outputs:
- new_coupling: bfloat16 [2, 4096, 2048], P('resp', 'item')
All inputs are finite; a program needn't handle non-finite values. No bound on the sum of `responses` on one device may be relied on, other than what follows from the above.
Results may differ from a plain program's by a relative error of at most 0.0035.
Values may be sent and summed in bfloat16 or wider, within the bound.
No kernel may reach another device: no remote copies, remote signals or barrier semaphores. Data moves between devices by JAX's collectives and lax.ppermute only.
A program may use at most 64 MiB of HBM per device.

v0:
```python
import math
import jax
import jax.numpy as jnp
from jax import lax
from jax.sharding import PartitionSpec as P

DRIFT = 0.01
DATA_RATIO = 900.0
NOISE_SCALE = math.sqrt(0.02)


def shards(coupling, noise, bias, responses, indices):
    couple = coupling[0]
    item_dev = couple.shape[0]
    n_resp = lax.axis_size("resp")
    n_item = lax.axis_size("item")
    sub_len = item_dev // n_resp
    inv_root = 1.0 / math.sqrt(item_dev * n_item)
    resp_idx = lax.axis_index("resp")
    item_idx = lax.axis_index("item")
    chosen = jnp.take(responses, indices, axis=0)
    spin_vals = (2 * chosen - 1).astype(jnp.bfloat16)
    summed = lax.psum_scatter(
        lax.dot_general(
            couple, spin_vals, (((0,), (1,)), ((), ())), preferred_element_type=jnp.float32
        ),
        "item",
        scatter_dimension=0,
        tiled=True,
    )
    own_start = resp_idx * sub_len
    diag_block = lax.dynamic_slice(couple, (own_start, item_idx * sub_len), (sub_len, sub_len))
    self_weight = jnp.diagonal(diag_block).astype(jnp.float32)
    spin_slice = lax.dynamic_slice_in_dim(spin_vals, own_start, sub_len, 1).T
    own_spin = spin_slice.astype(jnp.float32)
    own_answer = lax.dynamic_slice_in_dim(chosen, own_start, sub_len, 1).astype(jnp.float32).T
    fields = (summed - self_weight[:, None] * own_spin) * inv_root + bias[0][:, None]
    residual = (own_answer - jax.nn.sigmoid(fields)).astype(jnp.bfloat16)
    gathered = lax.all_gather(residual, "item", axis=0, tiled=True)
    tiles = jnp.einsum(
        "brt,kub->rktu",
        spin_vals.reshape(-1, n_resp, sub_len),
        gathered.reshape(n_item, sub_len, -1),
        preferred_element_type=jnp.float32,
    )
    flat_tiles = tiles.reshape(n_resp, n_item, sub_len * sub_len)
    moved = lax.all_to_all(
        lax.all_to_all(flat_tiles, "resp", split_axis=0, concat_axis=0, tiled=True),
        "item",
        split_axis=1,
        concat_axis=1,
        tiled=True,
    )
    own_part = tiles.transpose(0, 2, 1, 3).reshape(item_dev, n_item * sub_len)
    mirror = (
        moved.reshape(n_resp, n_item, sub_len, sub_len)
        .transpose(0, 3, 1, 2)
        .reshape(item_dev, n_item * sub_len)
    )
    row_ids = lax.broadcasted_iota(jnp.int32, (item_dev, n_item * sub_len), 0)
    col_ids = lax.broadcasted_iota(jnp.int32, (item_dev, n_item * sub_len), 1)
    on_diag = (
        (col_ids == item_idx * sub_len + row_ids - own_start)
        & (row_ids >= own_start)
        & (row_ids < own_start + sub_len)
    )
    gradient = jnp.where(on_diag, jnp.float32(0.0), own_part + mirror) * inv_root
    current = couple.astype(jnp.float32)
    updated = (
        current
        + DRIFT * (DATA_RATIO * gradient - current)
        + NOISE_SCALE * noise[0].astype(jnp.float32)
    )
    return updated.astype(jnp.bfloat16)[None]


def solution(mesh):
    return jax.shard_map(
        shards,
        mesh=mesh,
        in_specs=(
            P("resp", "item", None),
            P("resp", "item", None),
            P("item", "resp"),
            P(None, "item"),
            P(),
        ),
        out_specs=P("resp", "item", None),
        check_vma=False,
    )
```

profile of v0, /device:TPU:11, one launch (start us, length us, event | category | flops | bytes accessed | tf_op | source)
XLA Modules:
  0.0 247.9 jit_solution(4028890291314251297)
XLA Ops:
  6.5 0.8 compare_select_fusion
  7.3 0.7 compare_and_fusion
  8.0 1.6 gather_fusion
  9.6 0.9 add_convert_fusion
  10.6 2.7 %convolution_bitcast_fusion = f32[2048,512]{0,1:T(8,128)} fusion(bf16[512,256]{1,0:T(8,128)(2,1)S(1)} %get-tuple-element.5, bf16[1,256,2048]{2,1,0:T(8,128)(2,1)S(1)} %copy-done.1), kind=kOutput, calls=%fused_computation.2 | convolution fusion | flops 536870912 | bytes 5505024 | tf_op jit(solution)/shard_map/dot_general | solution.py:24
  13.2 0.0 reduce-scatter.2.cloned.1.call-update
  13.3 0.0 all-gather.2.cloned.1.call-start
  13.4 1.5 gather_fusion.1
  14.9 69.9 %reduce-scatter.2.cloned.1.call-done = f32[128,512]{0,1:T(8,128)} async-done(((f32[2048,512]{0,1:T(8,128)}), f32[128,512]{0,1:T(8,128)}) %reduce-scatter.2.cloned.1.call-update) | async-done | bytes 262160 | tf_op jit(solution)/shard_map/reduce_scatter | solution.py:23
  84.8 1.7 fusion.15
  86.5 43.1 %all-gather.2.cloned.1.call-done = bf16[2048,512]{0,1:T(8,128)(2,1)} async-done(((bf16[128,512]{0,1:T(8,128)(2,1)}), bf16[2048,512]{0,1:T(8,128)(2,1)}) %all-gather.2.cloned.1.call-update) | async-done | bytes 2097168 | tf_op jit(solution)/shard_map/all_gather | solution.py:39
  129.6 3.9 %copy.19 = bf16[2048,512]{1,0:T(8,128)(2,1)} copy(bf16[2048,512]{0,1:T(8,128)(2,1)} %all-gather.2.cloned.1.call-done) | data formatting | bytes 4194304 | tf_op jit(solution)/shard_map/reshape | solution.py:43
  133.5 2.3 fusion.6
  135.8 1.8 copy.15
  137.7 2.7 %reshape.138 = f32[2,16,16384]{2,1,0:T(8,128)} reshape(f32[2,16,128,128]{3,2,1,0:T(8,128)} %copy.15) | data formatting | bytes 4194304 | tf_op jit(solution)/shard_map/reshape | solution.py:46
  140.4 28.5 %all_to_all.10 = f32[2,16,16384]{2,1,0:T(8,128)S(1)} all-to-all(f32[2,16,16384]{2,1,0:T(8,128)} %reshape.138), channel_id=1, replica_groups=mesh['resp'=2,'item'=16] {'resp'}, dimensions={0} | all-to-all | bytes 4194304 | tf_op jit(solution)/shard_map/all_to_all | solution.py:48
  168.9 2.9 %copy.16 = f32[2,16,16384]{2,0,1:T(2,128)} copy(f32[2,16,16384]{2,1,0:T(8,128)S(1)} %all_to_all.10) | data formatting | bytes 4194304 | tf_op jit(solution)/shard_map/all_to_all | solution.py:48
  171.8 5.8 %all-to-all-start.1 = ((f32[2,16,16384]{2,0,1:T(2,128)}), f32[2,16,16384]{2,0,1:T(2,128)}, u32[]{:S(2)}, u32[]{:S(2)}) async-start(f32[2,16,16384]{2,0,1:T(2,128)} %copy.16), calls=%async_computation.2 | async-start | bytes 4194304 | tf_op jit(solution)/shard_map/all_to_all | solution.py:47
  177.7 47.5 %all-to-all-done.1 = f32[2,16,16384]{2,0,1:T(2,128)} async-done(((f32[2,16,16384]{2,0,1:T(2,128)}), f32[2,16,16384]{2,0,1:T(2,128)}, u32[]{:S(2)}, u32[]{:S(2)}) %all-to-all-start.1) | async-done | bytes 2097184 | tf_op jit(solution)/shard_map/all_to_all | solution.py:47
  225.2 4.0 %reshape.139 = f32[2,16,128,128]{3,2,0,1:T(8,128)} reshape(f32[2,16,16384]{2,0,1:T(2,128)} %all-to-all-done.1) | data formatting | bytes 4194304 | tf_op jit(solution)/shard_map/reshape | solution.py:56
  229.2 3.2 %bitcast_add_fusion = f32[2,128,16,128]{1,3,0,2:T(8,128)} fusion(f32[2,16,128,128]{3,2,0,1:T(8,128)} %reshape.139, f32[16,128,2,128]{3,1,2,0:T(8,128)S(1)} %fusion.6), kind=kLoop, calls=%fused_computation.8 | loop fusion | flops 524288 | bytes 6291456 | tf_op jit(solution)/shard_map/add | solution.py:67
  232.4 3.1 %copy.17 = f32[2,128,16,128]{3,2,1,0:T(8,128)} copy(f32[2,128,16,128]{1,3,0,2:T(8,128)} %bitcast_add_fusion) | data formatting | bytes 4194304 | tf_op jit(solution)/shard_map/add | solution.py:67
  235.5 1.7 add.87
  237.2 3.9 %fusion.2 = bf16[1,256,2048]{2,1,0:T(8,128)(2,1)} fusion(bf16[1,256,2048]{2,1,0:T(8,128)(2,1)} %param.5, bf16[1,256,2048]{2,1,0:T(8,128)(2,1)} %param.6, f32[1,256,2048]{2,1,0:T(8,128)S(1)} %add.87, s32[256]{0:T(256)S(1)} %add_subtract_fusion, pred[256]{0:T(512)(128)(4,1)S(1)} %get-tuple-element.7, pred[256]{0:T(512)(128)(4,1)S(1)} %get-tuple-element.8), kind=kLoop, calls=%fused_computation.7 | loop fusion | flops 6815744 | bytes 5244416 | tf_op jit(solution)/shard_map/convert_element_type | solution.py:74
  (16 shorter events, 0.1 us)
Async XLA Ops:
  6.5 1.5 copy-start
  6.5 78.2 %reduce-scatter.2.cloned.1.call-start = ((), (), s32[]{:S(2)}) async-start(), calls=%async_computation.3 | async-start | bytes 4456448 | tf_op jit(solution)/shard_map/reduce_scatter | solution.py:23
  8.0 2.5 %copy-start.1 = (bf16[1,256,2048]{2,1,0:T(8,128)(2,1)S(1)}, bf16[1,256,2048]{2,1,0:T(8,128)(2,1)}, u32[]{:S(2)}) copy-start(bf16[1,256,2048]{2,1,0:T(8,128)(2,1)} %param.5) | copy-start | bytes 3145732
  13.2 71.5 %copy-start.2 = (s32[512,256]{1,0:T(8,128)S(1)}, s32[512,256]{1,0:T(8,128)}, u32[]{:S(2)}) copy-start(s32[512,256]{1,0:T(8,128)} %get-tuple-element.6) | copy-start | bytes 1572868
  13.2 71.5 %copy-start.3 = (f32[1,128]{1,0:T(1,128)S(1)}, f32[1,128]{1,0:T(1,128)}, u32[]{:S(2)}) copy-start(f32[1,128]{1,0:T(1,128)} %param.7) | copy-start | bytes 1540
  13.3 116.3 %all-gather.2.cloned.1.call-start = ((), (), s32[]{:S(2)}) async-start(), calls=%async_computation.4 | async-start | bytes 2228224 | tf_op jit(solution)/shard_map/all_gather | solution.py:39
  171.8 53.4 %all-to-all-start.1 = ((f32[2,16,16384]{2,0,1:T(2,128)}), f32[2,16,16384]{2,0,1:T(2,128)}, u32[]{:S(2)}, u32[]{:S(2)}) async-start(f32[2,16,16384]{2,0,1:T(2,128)} %copy.16), calls=%async_computation.2 | async-start | bytes 4194304 | tf_op jit(solution)/shard_map/all_to_all | solution.py:47
Sparse Core Ops, SparseCore 0:
  13.4 71.3 reduce-scatter.1
  87.1 42.4 all-gather.1
where the time goes:
time: 248 us
  waiting for transfers between devices  161 us (65%)
  blocking collectives  28.5 us (11%)
  local copies, waits for them, and re-layouts  23.4 us (9%)
  between operations  13.5 us (5%)
  other arithmetic  11.2 us (5%)
  starting transfers between devices  5.89 us (2%)
  matrix products  4.96 us (2%)
    reduce_scatter x1, waiting for transfers between devices, shards(): lax.psum_scatter(lax.dot_general(couple, spin_vals, (((0,), (1,)), ((), (...  69.9 us
    all_to_all x1, waiting for transfers between devices, shards(): lax.all_to_all(lax.all_to_all(flat_tiles, 'resp', split_axis=0, concat_ax...  47.5 us
    all_gather x1, waiting for transfers between devices, shards(): gathered = lax.all_gather(residual, 'item', axis=0, tiled=True)  43.1 us
    all_to_all x1, blocking collectives, shards(): lax.all_to_all(flat_tiles, 'resp', split_axis=0, concat_axis=0, tiled=True)  28.5 us
    all_to_all x1, starting transfers between devices, shards(): lax.all_to_all(lax.all_to_all(flat_tiles, 'resp', split_axis=0, concat_ax...  5.85 us
  transfers between devices with their start and end apart: 3, of which 3 were waited for; matrix products, arithmetic and copies ran while one was open for 1% of the time, Pallas kernels for 0%

commit v1 on v0

--- a/solution.py
+++ b/solution.py
@@ -36,7 +36,16 @@
     own_answer = lax.dynamic_slice_in_dim(chosen, own_start, sub_len, 1).astype(jnp.float32).T
     fields = (summed - self_weight[:, None] * own_spin) * inv_root + bias[0][:, None]
     residual = (own_answer - jax.nn.sigmoid(fields)).astype(jnp.bfloat16)
-    gathered = lax.all_gather(residual, "item", axis=0, tiled=True)
+    ways = lax.axis_size("item")
+    up = [(d, (d + 1) % ways) for d in range(ways)]
+    down = [(d, (d - 1) % ways) for d in range(ways)]
+    earlier, later = ([residual], [residual])
+    for _ in range(ways // 2):
+        earlier.append(lax.ppermute(earlier[-1], "item", up))
+    for _ in range((ways - 1) // 2):
+        later.append(lax.ppermute(later[-1], "item", down))
+    line = jnp.concatenate([*earlier[::-1], *later[1:]], axis=0)
+    gathered = jnp.roll(line, (lax.axis_index("item") - ways // 2) * residual.shape[0], axis=0)
     tiles = jnp.einsum(
         "brt,kub->rktu",
         spin_vals.reshape(-1, n_resp, sub_len),

time: 248 us -> 259 us (1.044)
  starting transfers between devices: 5.89 us -> 42.5 us
  waiting for transfers between devices: 161 us -> 136 us
    all_gather x1 -> x0, waiting for transfers between devices: 43.1 us -> none  [shards(): gathered = lax.all_gather(residual, 'item', axis=0, tiled=True)]
    ppermute x0 -> x15, starting transfers between devices: none -> 26.9 us  [the longest x8 26.9 us: shards(): earlier.append(lax.ppermute(earlier[-1], 'item', up))]
    ppermute x0 -> x15, waiting for transfers between devices: none -> 18.2 us  [the longest x8 15.5 us: shards(): earlier.append(lax.ppermute(earlier[-1], 'item', up))]
    all_to_all x1, starting transfers between devices: 5.85 us -> 15.6 us  [shards(): lax.all_to_all(lax.all_to_all(flat_tiles, 'resp', split_axis=0, concat_ax...]
    reshape x1 -> x0, local copies, waits for them, and re-layouts: 3.92 us -> none  [shards(): gathered.reshape(n_item, sub_len, -1)]
    dynamic_slice x0 -> x2, local copies, waits for them, and re-layouts: none -> 2.78 us  [shards(): jnp.roll(line, (lax.axis_index('item') - ways // 2) * residual.shape[0],...]
  transfers between devices with their start and end apart: 3 -> 17, of which waited for: 3 -> 11; matrix products, arithmetic and copies ran while one was open for 1% -> 1% of each run, Pallas kernels for 0% -> 0%
where the time goes in v1:
time: 259 us
  waiting for transfers between devices  136 us (53%)
  starting transfers between devices  42.5 us (16%)
  blocking collectives  28.1 us (11%)
  local copies, waits for them, and re-layouts  23.4 us (9%)
  between operations  13.8 us (5%)
  other arithmetic  10.6 us (4%)
  matrix products  4.95 us (2%)
    reduce_scatter x1, waiting for transfers between devices, shards(): lax.psum_scatter(lax.dot_general(couple, spin_vals, (((0,), (1,)), ((), (...  70 us
    all_to_all x1, waiting for transfers between devices, shards(): lax.all_to_all(lax.all_to_all(flat_tiles, 'resp', split_axis=0, concat_ax...  47.5 us
    all_to_all x1, blocking collectives, shards(): lax.all_to_all(flat_tiles, 'resp', split_axis=0, concat_axis=0, tiled=True)  28.1 us
    ppermute x8, starting transfers between devices, shards(): earlier.append(lax.ppermute(earlier[-1], 'item', up))  26.9 us
    all_to_all x1, starting transfers between devices, shards(): lax.all_to_all(lax.all_to_all(flat_tiles, 'resp', split_axis=0, concat_ax...  15.6 us
    ppermute x8, waiting for transfers between devices, shards(): earlier.append(lax.ppermute(earlier[-1], 'item', up))  15.5 us
  transfers between devices with their start and end apart: 17, of which 11 were waited for; matrix products, arithmetic and copies ran while one was open for 1% of the time, Pallas kernels for 0%

profile of v1, /device:TPU:11, one launch (start us, length us, event | category | flops | bytes accessed | tf_op | source)
XLA Modules:
  0.0 259.0 jit_solution(17446484577306274996)
XLA Ops:
  10.6 2.7 %convolution_bitcast_fusion = f32[2048,512]{0,1:T(8,128)} fusion(bf16[512,256]{1,0:T(8,128)(2,1)S(1)} %get-tuple-element.5, bf16[1,256,2048]{2,1,0:T(8,128)(2,1)S(1)} %copy-done.1), kind=kOutput, calls=%fused_computation.2 | convolution fusion | flops 536870912 | bytes 5505024 | tf_op jit(solution)/shard_map/dot_general | solution.py:24
  14.9 70.0 %reduce-scatter.2.cloned.1.call-done = f32[128,512]{0,1:T(8,128)} async-done(((f32[2048,512]{0,1:T(8,128)}), f32[128,512]{0,1:T(8,128)}) %reduce-scatter.2.cloned.1.call-update) | async-done | bytes 262160 | tf_op jit(solution)/shard_map/reduce_scatter | solution.py:23
  86.0 2.9 %collective-permute-start = (bf16[128,512]{0,1:T(8,128)(2,1)S(1)}, bf16[128,512]{0,1:T(8,128)(2,1)S(1)}, u32[]{:S(2)}, u32[]{:S(2)}) collective-permute-start(bf16[128,512]{0,1:T(8,128)(2,1)S(1)} %fusion.15), channel_id=1, source_target_pairs={{0,1},{1,2},{2,3},{3,4},{4,5},{5,6},{6,7},{7,8},{8,9},{9,10},{10,1... | collective-permute-start | bytes 393224 | tf_op jit(solution)/shard_map/ppermute | solution.py:44
  88.9 1.9 collective-permute-done
  90.8 3.3 %collective-permute-start.1 = (bf16[128,512]{0,1:T(8,128)(2,1)S(1)}, bf16[128,512]{0,1:T(8,128)(2,1)S(1)}, u32[]{:S(2)}, u32[]{:S(2)}) collective-permute-start(bf16[128,512]{0,1:T(8,128)(2,1)S(1)} %collective-permute-done), channel_id=1, source_target_pairs={{0,1},{1,2},{2,3},{3,4},{4,5},{5,6},{6,7},{7,8},{8,9},{9,10},{10,1... | collective-permute-start | bytes 393224 | tf_op jit(solution)/shard_map/ppermute | solution.py:44
  94.2 1.9 collective-permute-done.1
  96.1 3.4 %collective-permute-start.2 = (bf16[128,512]{0,1:T(8,128)(2,1)S(1)}, bf16[128,512]{0,1:T(8,128)(2,1)S(1)}, u32[]{:S(2)}, u32[]{:S(2)}) collective-permute-start(bf16[128,512]{0,1:T(8,128)(2,1)S(1)} %collective-permute-done.1), channel_id=1, source_target_pairs={{0,1},{1,2},{2,3},{3,4},{4,5},{5,6},{6,7},{7,8},{8,9},{9,10},{10,1... | collective-permute-start | bytes 393224 | tf_op jit(solution)/shard_map/ppermute | solution.py:44
  101.5 3.4 %collective-permute-start.3 = (bf16[128,512]{0,1:T(8,128)(2,1)S(1)}, bf16[128,512]{0,1:T(8,128)(2,1)S(1)}, u32[]{:S(2)}, u32[]{:S(2)}) collective-permute-start(bf16[128,512]{0,1:T(8,128)(2,1)S(1)} %collective-permute-done.2), channel_id=1, source_target_pairs={{0,1},{1,2},{2,3},{3,4},{4,5},{5,6},{6,7},{7,8},{8,9},{9,10},{10,1... | collective-permute-start | bytes 393224 | tf_op jit(solution)/shard_map/ppermute | solution.py:44
  106.9 3.4 %collective-permute-start.4 = (bf16[128,512]{0,1:T(8,128)(2,1)S(1)}, bf16[128,512]{0,1:T(8,128)(2,1)S(1)}, u32[]{:S(2)}, u32[]{:S(2)}) collective-permute-start(bf16[128,512]{0,1:T(8,128)(2,1)S(1)} %collective-permute-done.3), channel_id=1, source_target_pairs={{0,1},{1,2},{2,3},{3,4},{4,5},{5,6},{6,7},{7,8},{8,9},{9,10},{10,1... | collective-permute-start | bytes 393224 | tf_op jit(solution)/shard_map/ppermute | solution.py:44
  112.3 3.4 %collective-permute-start.5 = (bf16[128,512]{0,1:T(8,128)(2,1)S(1)}, bf16[128,512]{0,1:T(8,128)(2,1)S(1)}, u32[]{:S(2)}, u32[]{:S(2)}) collective-permute-start(bf16[128,512]{0,1:T(8,128)(2,1)S(1)} %collective-permute-done.4), channel_id=1, source_target_pairs={{0,1},{1,2},{2,3},{3,4},{4,5},{5,6},{6,7},{7,8},{8,9},{9,10},{10,1... | collective-permute-start | bytes 393224 | tf_op jit(solution)/shard_map/ppermute | solution.py:44
  117.7 3.4 %collective-permute-start.6 = (bf16[128,512]{0,1:T(8,128)(2,1)S(1)}, bf16[128,512]{0,1:T(8,128)(2,1)S(1)}, u32[]{:S(2)}, u32[]{:S(2)}) collective-permute-start(bf16[128,512]{0,1:T(8,128)(2,1)S(1)} %collective-permute-done.5), channel_id=1, source_target_pairs={{0,1},{1,2},{2,3},{3,4},{4,5},{5,6},{6,7},{7,8},{8,9},{9,10},{10,1... | collective-permute-start | bytes 393224 | tf_op jit(solution)/shard_map/ppermute | solution.py:44
  123.1 3.4 %collective-permute-start.7 = (bf16[128,512]{0,1:T(8,128)(2,1)S(1)}, bf16[128,512]{0,1:T(8,128)(2,1)S(1)}, u32[]{:S(2)}, u32[]{:S(2)}) collective-permute-start(bf16[128,512]{0,1:T(8,128)(2,1)S(1)} %collective-permute-done.6), channel_id=1, source_target_pairs={{0,1},{1,2},{2,3},{3,4},{4,5},{5,6},{6,7},{7,8},{8,9},{9,10},{10,1... | collective-permute-start | bytes 393224 | tf_op jit(solution)/shard_map/ppermute | solution.py:44
  129.2 2.7 %collective-permute-done.14 = bf16[128,512]{0,1:T(8,128)(2,1)S(1)} collective-permute-done((bf16[128,512]{0,1:T(8,128)(2,1)S(1)}, bf16[128,512]{0,1:T(8,128)(2,1)S(1)}, u32[]{:S(2)}, u32[]{:S(2)}) %collective-permute-start.14) | collective-permute-done | bytes 131104 | tf_op jit(solution)/shard_map/ppermute | solution.py:46
  132.9 2.5 copy.12
  135.4 2.3 fusion.6
  139.6 2.7 %reshape.138 = f32[2,16,16384]{2,1,0:T(8,128)} reshape(f32[2,16,128,128]{3,2,1,0:T(8,128)} %copy.14) | data formatting | bytes 4194304 | tf_op jit(solution)/shard_map/reshape | solution.py:55
  142.3 28.1 %all_to_all.10 = f32[2,16,16384]{2,1,0:T(8,128)S(1)} all-to-all(f32[2,16,16384]{2,1,0:T(8,128)} %reshape.138), channel_id=1, replica_groups=mesh['resp'=2,'item'=16] {'resp'}, dimensions={0} | all-to-all | bytes 4194304 | tf_op jit(solution)/shard_map/all_to_all | solution.py:57
  170.3 2.9 %copy.15 = f32[2,16,16384]{2,0,1:T(2,128)} copy(f32[2,16,16384]{2,1,0:T(8,128)S(1)} %all_to_all.10) | data formatting | bytes 4194304 | tf_op jit(solution)/shard_map/all_to_all | solution.py:57
  173.3 15.6 %all-to-all-start.1 = ((f32[2,16,16384]{2,0,1:T(2,128)}), f32[2,16,16384]{2,0,1:T(2,128)}, u32[]{:S(2)}, u32[]{:S(2)}) async-start(f32[2,16,16384]{2,0,1:T(2,128)} %copy.15), calls=%async_computation.2 | async-start | bytes 4194304 | tf_op jit(solution)/shard_map/all_to_all | solution.py:56
  188.9 47.5 %all-to-all-done.1 = f32[2,16,16384]{2,0,1:T(2,128)} async-done(((f32[2,16,16384]{2,0,1:T(2,128)}), f32[2,16,16384]{2,0,1:T(2,128)}, u32[]{:S(2)}, u32[]{:S(2)}) %all-to-all-start.1) | async-done | bytes 2097184 | tf_op jit(solution)/shard_map/all_to_all | solution.py:56
  236.4 4.0 %reshape.139 = f32[2,16,128,128]{3,2,0,1:T(8,128)} reshape(f32[2,16,16384]{2,0,1:T(2,128)} %all-to-all-done.1) | data formatting | bytes 4194304 | tf_op jit(solution)/shard_map/reshape | solution.py:65
  240.4 3.1 %bitcast_add_fusion = f32[2,128,16,128]{1,3,0,2:T(8,128)} fusion(f32[2,16,128,128]{3,2,0,1:T(8,128)} %reshape.139, f32[16,128,2,128]{3,1,2,0:T(8,128)S(1)} %fusion.6), kind=kLoop, calls=%fused_computation.8 | loop fusion | flops 524288 | bytes 6291456 | tf_op jit(solution)/shard_map/add | solution.py:76
  243.5 3.0 %copy.16 = f32[2,128,16,128]{3,2,1,0:T(8,128)} copy(f32[2,128,16,128]{1,3,0,2:T(8,128)} %bitcast_add_fusion) | data formatting | bytes 4194304 | tf_op jit(solution)/shard_map/add | solution.py:76
  248.3 3.9 %fusion.2 = bf16[1,256,2048]{2,1,0:T(8,128)(2,1)} fusion(bf16[1,256,2048]{2,1,0:T(8,128)(2,1)} %param.5, bf16[1,256,2048]{2,1,0:T(8,128)(2,1)} %param.6, f32[1,256,2048]{2,1,0:T(8,128)S(1)} %add.100, s32[256]{0:T(256)S(1)} %add_subtract_fusion, pred[256]{0:T(512)(128)(4,1)S(1)} %iota_compare_fusion.1, pred[256]{0:T(512)(128)(4,1)S(1)} %iota_compare_fusion.2), kind=kLoop, calls=%fused_computation.7 | loop fusion | flops 6815744 | bytes 5244416 | tf_op jit(solution)/shard_map/convert_element_type | solution.py:83
  (77 shorter events, 23.4 us)
Async XLA Ops:
  6.5 1.5 copy-start
  6.5 4.1 %copy-start.1 = (bf16[1,256,2048]{2,1,0:T(8,128)(2,1)S(1)}, bf16[1,256,2048]{2,1,0:T(8,128)(2,1)}, u32[]{:S(2)}) copy-start(bf16[1,256,2048]{2,1,0:T(8,128)(2,1)} %param.5) | copy-start | bytes 3145732
  6.5 78.4 %reduce-scatter.2.cloned.1.call-start = ((), (), s32[]{:S(2)}) async-start(), calls=%async_computation.3 | async-start | bytes 4456448 | tf_op jit(solution)/shard_map/reduce_scatter | solution.py:23
  13.3 71.6 %copy-start.2 = (s32[512,256]{1,0:T(8,128)S(1)}, s32[512,256]{1,0:T(8,128)}, u32[]{:S(2)}) copy-start(s32[512,256]{1,0:T(8,128)} %get-tuple-element.6) | copy-start | bytes 1572868
  13.3 71.6 %copy-start.3 = (f32[1,128]{1,0:T(1,128)S(1)}, f32[1,128]{1,0:T(1,128)}, u32[]{:S(2)}) copy-start(f32[1,128]{1,0:T(1,128)} %param.7) | copy-start | bytes 1540
  86.0 4.8 %collective-permute-start = (bf16[128,512]{0,1:T(8,128)(2,1)S(1)}, bf16[128,512]{0,1:T(8,128)(2,1)S(1)}, u32[]{:S(2)}, u32[]{:S(2)}) collective-permute-start(bf16[128,512]{0,1:T(8,128)(2,1)S(1)} %fusion.15), channel_id=1, source_target_pairs={{0,1},{1,2},{2,3},{3,4},{4,5},{5,6},{6,7},{7,8},{8,9},{9,10},{10,1... | collective-permute-start | bytes 393224 | tf_op jit(solution)/shard_map/ppermute | solution.py:44
  90.8 5.3 %collective-permute-start.1 = (bf16[128,512]{0,1:T(8,128)(2,1)S(1)}, bf16[128,512]{0,1:T(8,128)(2,1)S(1)}, u32[]{:S(2)}, u32[]{:S(2)}) collective-permute-start(bf16[128,512]{0,1:T(8,128)(2,1)S(1)} %collective-permute-done), channel_id=1, source_target_pairs={{0,1},{1,2},{2,3},{3,4},{4,5},{5,6},{6,7},{7,8},{8,9},{9,10},{10,1... | collective-permute-start | bytes 393224 | tf_op jit(solution)/shard_map/ppermute | solution.py:44
  94.2 5.4 %collective-permute-start.8 = (bf16[128,512]{0,1:T(8,128)(2,1)S(1)}, bf16[128,512]{0,1:T(8,128)(2,1)S(1)}, u32[]{:S(2)}, u32[]{:S(2)}) collective-permute-start(bf16[128,512]{0,1:T(8,128)(2,1)S(1)} %fusion.15), channel_id=1, source_target_pairs={{0,15},{1,0},{2,1},{3,2},{4,3},{5,4},{6,5},{7,6},{8,7},{9,8},{10,9... | collective-permute-start | bytes 393224 | tf_op jit(solution)/shard_map/ppermute | solution.py:46
  96.1 5.4 %collective-permute-start.2 = (bf16[128,512]{0,1:T(8,128)(2,1)S(1)}, bf16[128,512]{0,1:T(8,128)(2,1)S(1)}, u32[]{:S(2)}, u32[]{:S(2)}) collective-permute-start(bf16[128,512]{0,1:T(8,128)(2,1)S(1)} %collective-permute-done.1), channel_id=1, source_target_pairs={{0,1},{1,2},{2,3},{3,4},{4,5},{5,6},{6,7},{7,8},{8,9},{9,10},{10,1... | collective-permute-start | bytes 393224 | tf_op jit(solution)/shard_map/ppermute | solution.py:44
  99.6 5.4 %collective-permute-start.9 = (bf16[128,512]{0,1:T(8,128)(2,1)S(1)}, bf16[128,512]{0,1:T(8,128)(2,1)S(1)}, u32[]{:S(2)}, u32[]{:S(2)}) collective-permute-start(bf16[128,512]{0,1:T(8,128)(2,1)S(1)} %collective-permute-done.8), channel_id=1, source_target_pairs={{0,15},{1,0},{2,1},{3,2},{4,3},{5,4},{6,5},{7,6},{8,7},{9,8},{10,9... | collective-permute-start | bytes 393224 | tf_op jit(solution)/shard_map/ppermute | solution.py:46
  101.5 5.4 %collective-permute-start.3 = (bf16[128,512]{0,1:T(8,128)(2,1)S(1)}, bf16[128,512]{0,1:T(8,128)(2,1)S(1)}, u32[]{:S(2)}, u32[]{:S(2)}) collective-permute-start(bf16[128,512]{0,1:T(8,128)(2,1)S(1)} %collective-permute-done.2), channel_id=1, source_target_pairs={{0,1},{1,2},{2,3},{3,4},{4,5},{5,6},{6,7},{7,8},{8,9},{9,10},{10,1... | collective-permute-start | bytes 393224 | tf_op jit(solution)/shard_map/ppermute | solution.py:44
  105.0 5.4 %collective-permute-start.10 = (bf16[128,512]{0,1:T(8,128)(2,1)S(1)}, bf16[128,512]{0,1:T(8,128)(2,1)S(1)}, u32[]{:S(2)}, u32[]{:S(2)}) collective-permute-start(bf16[128,512]{0,1:T(8,128)(2,1)S(1)} %collective-permute-done.9), channel_id=1, source_target_pairs={{0,15},{1,0},{2,1},{3,2},{4,3},{5,4},{6,5},{7,6},{8,7},{9,8},{10,9... | collective-permute-start | bytes 393224 | tf_op jit(solution)/shard_map/ppermute | solution.py:46
  106.9 5.4 %collective-permute-start.4 = (bf16[128,512]{0,1:T(8,128)(2,1)S(1)}, bf16[128,512]{0,1:T(8,128)(2,1)S(1)}, u32[]{:S(2)}, u32[]{:S(2)}) collective-permute-start(bf16[128,512]{0,1:T(8,128)(2,1)S(1)} %collective-permute-done.3), channel_id=1, source_target_pairs={{0,1},{1,2},{2,3},{3,4},{4,5},{5,6},{6,7},{7,8},{8,9},{9,10},{10,1... | collective-permute-start | bytes 393224 | tf_op jit(solution)/shard_map/ppermute | solution.py:44
  110.3 5.4 %collective-permute-start.11 = (bf16[128,512]{0,1:T(8,128)(2,1)S(1)}, bf16[128,512]{0,1:T(8,128)(2,1)S(1)}, u32[]{:S(2)}, u32[]{:S(2)}) collective-permute-start(bf16[128,512]{0,1:T(8,128)(2,1)S(1)} %collective-permute-done.10), channel_id=1, source_target_pairs={{0,15},{1,0},{2,1},{3,2},{4,3},{5,4},{6,5},{7,6},{8,7},{9,8},{10,9... | collective-permute-start | bytes 393224 | tf_op jit(solution)/shard_map/ppermute | solution.py:46
  112.3 5.4 %collective-permute-start.5 = (bf16[128,512]{0,1:T(8,128)(2,1)S(1)}, bf16[128,512]{0,1:T(8,128)(2,1)S(1)}, u32[]{:S(2)}, u32[]{:S(2)}) collective-permute-start(bf16[128,512]{0,1:T(8,128)(2,1)S(1)} %collective-permute-done.4), channel_id=1, source_target_pairs={{0,1},{1,2},{2,3},{3,4},{4,5},{5,6},{6,7},{7,8},{8,9},{9,10},{10,1... | collective-permute-start | bytes 393224 | tf_op jit(solution)/shard_map/ppermute | solution.py:44
  115.7 5.4 %collective-permute-start.12 = (bf16[128,512]{0,1:T(8,128)(2,1)S(1)}, bf16[128,512]{0,1:T(8,128)(2,1)S(1)}, u32[]{:S(2)}, u32[]{:S(2)}) collective-permute-start(bf16[128,512]{0,1:T(8,128)(2,1)S(1)} %collective-permute-done.11), channel_id=1, source_target_pairs={{0,15},{1,0},{2,1},{3,2},{4,3},{5,4},{6,5},{7,6},{8,7},{9,8},{10,9... | collective-permute-start | bytes 393224 | tf_op jit(solution)/shard_map/ppermute | solution.py:46
  117.7 5.4 %collective-permute-start.6 = (bf16[128,512]{0,1:T(8,128)(2,1)S(1)}, bf16[128,512]{0,1:T(8,128)(2,1)S(1)}, u32[]{:S(2)}, u32[]{:S(2)}) collective-permute-start(bf16[128,512]{0,1:T(8,128)(2,1)S(1)} %collective-permute-done.5), channel_id=1, source_target_pairs={{0,1},{1,2},{2,3},{3,4},{4,5},{5,6},{6,7},{7,8},{8,9},{9,10},{10,1... | collective-permute-start | bytes 393224 | tf_op jit(solution)/shard_map/ppermute | solution.py:44
  121.1 5.4 %collective-permute-start.13 = (bf16[128,512]{0,1:T(8,128)(2,1)S(1)}, bf16[128,512]{0,1:T(8,128)(2,1)S(1)}, u32[]{:S(2)}, u32[]{:S(2)}) collective-permute-start(bf16[128,512]{0,1:T(8,128)(2,1)S(1)} %collective-permute-done.12), channel_id=1, source_target_pairs={{0,15},{1,0},{2,1},{3,2},{4,3},{5,4},{6,5},{7,6},{8,7},{9,8},{10,9... | collective-permute-start | bytes 393224 | tf_op jit(solution)/shard_map/ppermute | solution.py:46
  123.1 5.4 %collective-permute-start.7 = (bf16[128,512]{0,1:T(8,128)(2,1)S(1)}, bf16[128,512]{0,1:T(8,128)(2,1)S(1)}, u32[]{:S(2)}, u32[]{:S(2)}) collective-permute-start(bf16[128,512]{0,1:T(8,128)(2,1)S(1)} %collective-permute-done.6), channel_id=1, source_target_pairs={{0,1},{1,2},{2,3},{3,4},{4,5},{5,6},{6,7},{7,8},{8,9},{9,10},{10,1... | collective-permute-start | bytes 393224 | tf_op jit(solution)/shard_map/ppermute | solution.py:44
  126.5 5.3 %collective-permute-start.14 = (bf16[128,512]{0,1:T(8,128)(2,1)S(1)}, bf16[128,512]{0,1:T(8,128)(2,1)S(1)}, u32[]{:S(2)}, u32[]{:S(2)}) collective-permute-start(bf16[128,512]{0,1:T(8,128)(2,1)S(1)} %collective-permute-done.13), channel_id=1, source_target_pairs={{0,15},{1,0},{2,1},{3,2},{4,3},{5,4},{6,5},{7,6},{8,7},{9,8},{10,9... | collective-permute-start | bytes 393224 | tf_op jit(solution)/shard_map/ppermute | solution.py:46
  173.3 63.1 %all-to-all-start.1 = ((f32[2,16,16384]{2,0,1:T(2,128)}), f32[2,16,16384]{2,0,1:T(2,128)}, u32[]{:S(2)}, u32[]{:S(2)}) async-start(f32[2,16,16384]{2,0,1:T(2,128)} %copy.15), calls=%async_computation.2 | async-start | bytes 4194304 | tf_op jit(solution)/shard_map/all_to_all | solution.py:56
Sparse Core Ops, SparseCore 0:
  13.4 71.4 reduce-scatter.1
